TPU v7x, 32 devices: a whole 2x2x4 slice. The times are simulated.
32 devices in a mesh: seq: 8 (over y, x, core), dp: 4 (over z).
Axes of the slice: x: 2, y: 2, z: 4, core: 2. Of those that a mesh axis runs over, the one named last changes fastest.
Arguments:
- tokens: bfloat16 [4, 1024, 2048], P('dp', 'seq'), may hold values from -6 to 6
- doc_lengths: int32 [4, 8], P('dp'), may hold values from 1 to 512, 1024 in all within a row
- query_weight: bfloat16 [2048, 2048], P(('seq', 'dp')), may hold values from -0.125 to 0.125
- key_weight: bfloat16 [512, 2048], P(('seq', 'dp')), may hold values from -0.125 to 0.125
- value_weight: bfloat16 [512, 2048], P(('seq', 'dp')), may hold values from -0.125 to 0.125
- output_weight: bfloat16 [2048, 2048], P(('seq', 'dp')), may hold values from -1 to 1
- gate_weight: bfloat16 [8192, 2048], P('seq'), may hold values from -0.125 to 0.125
- up_weight: bfloat16 [8192, 2048], P('seq'), may hold values from -0.125 to 0.125
- down_weight: bfloat16 [8192, 2048], P('seq'), may hold values from -0.0625 to 0.0625
- attn_gain: bfloat16 [2048], P(('seq', 'dp')), may hold values from 0.099609375 to 1.8984375
- mlp_gain: bfloat16 [2048], P(('seq', 'dp')), may hold values from 0.099609375 to 1.8984375
- cotangent: bfloat16 [4, 1024, 2048], P('dp', 'seq'), may hold values from -6 to 6
Outputs:
- output: bfloat16 [4, 1024, 2048], P('dp', 'seq')
- grad_tokens: bfloat16 [4, 1024, 2048], P('dp', 'seq')
- grad_query: float32 [2048, 2048], P(('seq', 'dp'))
- grad_key: float32 [512, 2048], P(('seq', 'dp'))
- grad_value: float32 [512, 2048], P(('seq', 'dp'))
- grad_output: float32 [2048, 2048], P(('seq', 'dp'))
- grad_gate: float32 [8192, 2048], P('seq')
- grad_up: float32 [8192, 2048], P('seq')
- grad_down: float32 [8192, 2048], P('seq')
- grad_attn_gain: float32 [2048], P(('seq', 'dp'))
- grad_mlp_gain: float32 [2048], P(('seq', 'dp'))
Inputs may be any that keep to these rules, and one draw needn't show every extreme that they name: `doc_lengths`: each sequence's 8 document lengths sum to 1024; its longest document has exactly 512 tokens.
All inputs are finite; a program needn't handle non-finite values.
Results may differ from a plain program's by a relative error of at most 0.015.
Values may be sent and summed in bfloat16 or wider, within the bound.
No kernel may reach another device: no remote copies, remote signals or barrier semaphores. Data moves between devices by JAX's collectives and lax.ppermute only.
A program may use at most 192 MiB of HBM per device.

v0:
```python
import math

import jax
import jax.numpy as jnp
from jax import lax
from jax.sharding import PartitionSpec as P

HEADS = 32
KV_HEADS = 8
HEAD_DIM = 64


norm_eps = 1e-05


def by_rows(left, weight_mat):
    return lax.dot_general(
        left, weight_mat, (((1,), (1,)), ((), ())), preferred_element_type=jnp.float32
    )


def by_tokens(left, right):
    return lax.dot_general(
        left, right, (((0,), (0,)), ((), ())), preferred_element_type=jnp.float32
    )


def rms_norm(values, gain_vec):
    return (
        values * lax.rsqrt(jnp.mean(values * values, axis=-1, keepdims=True) + norm_eps) * gain_vec
    )


def rope_tables(positions, head_size):
    half_size = head_size // 2
    exponent = jnp.arange(half_size, dtype=jnp.float32) * 2.0 / head_size
    inverse = 1.0 / 500000.0**exponent
    wavelen = 2.0 * math.pi / inverse
    scaled = jnp.where(wavelen > 8192.0, inverse / 32.0, inverse)
    smooth = (8192.0 / wavelen - 1.0) / 3.0
    smoothed = (1.0 - smooth) * scaled / 32.0 + smooth * scaled
    medium = (wavelen >= 2048.0) & (wavelen <= 8192.0)
    inverse = jnp.where(medium, smoothed, scaled)
    angles = positions.astype(jnp.float32)[:, None] * inverse[None, :]
    angles = jnp.concatenate([angles, angles], axis=-1)
    return (jnp.cos(angles), jnp.sin(angles))


def rotate(values, cos_tab, sin_tab):
    half_size = values.shape[-1] // 2
    turned = jnp.concatenate([-values[..., half_size:], values[..., :half_size]], axis=-1)
    return values * cos_tab[:, None, :] + turned * sin_tab[:, None, :]


def rotate_back(grads_in, cos_tab, sin_tab):
    half_size = grads_in.shape[-1] // 2
    scaled = grads_in * sin_tab[:, None, :]
    turned = jnp.concatenate([scaled[..., half_size:], -scaled[..., :half_size]], axis=-1)
    return grads_in * cos_tab[:, None, :] + turned


def doc_layout(doc_lens, total_len):
    doc_ends = jnp.cumsum(doc_lens, dtype=jnp.int32)
    places = jnp.arange(total_len, dtype=jnp.int32)
    passed = (places[:, None] >= doc_ends[None, :]).astype(jnp.int32)
    segment = jnp.sum(passed, axis=1, dtype=jnp.int32)
    position = places - jnp.sum(passed * doc_lens[None, :], axis=1, dtype=jnp.int32)
    return (segment, position)


def gate_grads(d_active, gate_val, up_val, sigmoid_val):
    d_gate = (d_active * up_val * sigmoid_val * (1.0 + gate_val * (1.0 - sigmoid_val))).astype(
        jnp.bfloat16
    )
    d_up = (d_active * gate_val * sigmoid_val).astype(jnp.bfloat16)
    return (d_gate, d_up)


def shards(
    tokens,
    doc_lengths,
    query_weight,
    key_weight,
    value_weight,
    output_weight,
    gate_weight,
    up_weight,
    down_weight,
    attn_gain,
    mlp_gain,
    cotangent,
):
    groups = lax.axis_size("seq")
    my_index = lax.axis_index("seq")
    local_len = tokens.shape[1]
    total_len = local_len * groups
    head_size = HEAD_DIM
    kv_count = KV_HEADS
    head_count = HEADS
    per_group = head_count // groups
    copies = groups // kv_count
    group_width = per_group * head_size
    block_len = min(512, total_len)
    score_scale = head_size ** (-0.5)
    inputs = tokens[0].astype(jnp.float32)
    cot_bf = cotangent[0]
    segment, position = doc_layout(doc_lengths[0], total_len)
    local_pos = lax.dynamic_slice_in_dim(position, my_index * local_len, local_len, 0)
    cos_tab, sin_tab = rope_tables(local_pos, head_size)
    query_all, key_all, value_all, output_all, attn_gain_all, mlp_gain_all = (
        lax.all_gather(query_weight, ("seq", "dp"), axis=0, tiled=True),
        lax.all_gather(key_weight, ("seq", "dp"), axis=0, tiled=True),
        lax.all_gather(value_weight, ("seq", "dp"), axis=0, tiled=True),
        lax.all_gather(output_weight, ("seq", "dp"), axis=0, tiled=True),
        lax.all_gather(attn_gain, ("seq", "dp"), axis=0, tiled=True),
        lax.all_gather(mlp_gain, ("seq", "dp"), axis=0, tiled=True),
    )
    normed, norm_one_back = jax.vjp(rms_norm, inputs, attn_gain_all.astype(jnp.float32))
    normed_bf = normed.astype(jnp.bfloat16)
    query_lin = by_rows(normed_bf, query_all).reshape(local_len, head_count, head_size)
    key_lin = by_rows(normed_bf, key_all).reshape(local_len, kv_count, head_size)
    value_bf = (
        by_rows(normed_bf, value_all).astype(jnp.bfloat16).reshape(local_len, kv_count, head_size)
    )
    query_send = (
        rotate(query_lin, cos_tab, sin_tab)
        .astype(jnp.bfloat16)
        .reshape(local_len, groups, group_width)
    )
    key_bf = rotate(key_lin, cos_tab, sin_tab).astype(jnp.bfloat16)
    pair_send = jnp.repeat(jnp.concatenate([key_bf, value_bf], axis=-1), copies, axis=1)
    query_heads, pair_heads = (
        lax.all_to_all(query_send, "seq", split_axis=1, concat_axis=0, tiled=True),
        lax.all_to_all(pair_send, "seq", split_axis=1, concat_axis=0, tiled=True),
    )
    query_blocks = query_heads.reshape(total_len // block_len, block_len, per_group, head_size)
    keys_here = pair_heads[:, 0, :head_size]
    values_here = pair_heads[:, 0, head_size:]
    key_place = jnp.arange(total_len, dtype=jnp.int32)
    starts = jnp.arange(0, total_len, block_len, dtype=jnp.int32)

    def block_scores(begin_at, query_blk):
        raw_scores = jnp.einsum(
            "qhd,kd->hqk", query_blk, keys_here, preferred_element_type=jnp.float32
        )
        row_place = begin_at + jnp.arange(block_len, dtype=jnp.int32)
        seg_blk = lax.dynamic_slice_in_dim(segment, begin_at, block_len, 0)
        allowed = (key_place[None, :] <= row_place[:, None]) & (
            segment[None, :] == seg_blk[:, None]
        )
        return jnp.where(allowed[None], raw_scores * score_scale, -1e30)

    def forward_block(packed):
        begin_at, query_blk = packed
        scores = block_scores(begin_at, query_blk)
        row_peak = jnp.max(scores, axis=-1, keepdims=True)
        log_total = row_peak + jnp.log(jnp.sum(jnp.exp(scores - row_peak), axis=-1, keepdims=True))
        soft_probs = jnp.exp(scores - log_total).astype(jnp.bfloat16)
        mixed_blk = jnp.einsum(
            "hqk,kd->qhd", soft_probs, values_here, preferred_element_type=jnp.float32
        )
        return (mixed_blk.astype(jnp.bfloat16), log_total[..., 0])

    mixed_blocks, log_totals = lax.map(forward_block, (starts, query_blocks))
    mixed_heads = mixed_blocks.reshape(total_len, 1, group_width)
    mixed = lax.all_to_all(mixed_heads, "seq", split_axis=0, concat_axis=1, tiled=True).reshape(
        local_len, head_count * head_size
    )
    hidden_state = inputs + by_rows(mixed, output_all)
    normed_two, norm_two_back = jax.vjp(rms_norm, hidden_state, mlp_gain_all.astype(jnp.float32))
    normed_two_bf = normed_two.astype(jnp.bfloat16)
    normed_all = lax.all_gather(normed_two_bf, "seq", axis=0, tiled=True)
    gate_val = by_rows(normed_all, gate_weight)
    up_val = by_rows(normed_all, up_weight)
    sigmoid_val = 1.0 / (1.0 + jnp.exp(-gate_val))
    active = (gate_val * sigmoid_val * up_val).astype(jnp.bfloat16)
    mlp_out = lax.psum_scatter(
        jnp.dot(active, down_weight, preferred_element_type=jnp.float32).astype(jnp.bfloat16),
        "seq",
        scatter_dimension=0,
        tiled=True,
    ).astype(jnp.float32)
    cot_all = lax.all_gather(cot_bf, "seq", axis=0, tiled=True)
    d_active = by_rows(cot_all, down_weight)
    d_gate, d_up = gate_grads(d_active, gate_val, up_val, sigmoid_val)
    grad_gate = by_tokens(d_gate, normed_all)
    grad_up = by_tokens(d_up, normed_all)
    grad_down = by_tokens(active, cot_all)
    d_normed_two = lax.psum_scatter(
        (
            jnp.dot(d_gate, gate_weight, preferred_element_type=jnp.float32)
            + jnp.dot(d_up, up_weight, preferred_element_type=jnp.float32)
        ).astype(jnp.bfloat16),
        "seq",
        scatter_dimension=0,
        tiled=True,
    ).astype(jnp.float32)
    grad_gate, grad_up, grad_down = (
        lax.psum(grad_gate.astype(jnp.bfloat16), "dp").astype(jnp.float32),
        lax.psum(grad_up.astype(jnp.bfloat16), "dp").astype(jnp.float32),
        lax.psum(grad_down.astype(jnp.bfloat16), "dp").astype(jnp.float32),
    )
    result = (hidden_state + mlp_out).astype(jnp.bfloat16)
    d_hidden_part, grad_mlp_gain = norm_two_back(d_normed_two)
    d_hidden = cot_bf.astype(jnp.float32) + d_hidden_part
    d_branch = d_hidden.astype(jnp.bfloat16)
    d_mixed = jnp.dot(d_branch, output_all, preferred_element_type=jnp.float32).astype(jnp.bfloat16)
    d_mixed_heads = lax.all_to_all(
        d_mixed.reshape(local_len, groups, group_width),
        "seq",
        split_axis=1,
        concat_axis=0,
        tiled=True,
    )
    d_mixed_blocks = d_mixed_heads.reshape(total_len // block_len, block_len, per_group, head_size)

    def backward_block(carry, packed):
        d_keys, d_values = carry
        begin_at, query_blk, d_mixed_blk, log_blk = packed
        scores = block_scores(begin_at, query_blk)
        soft_probs = jnp.exp(scores - log_blk[..., None])
        d_probs = jnp.einsum(
            "qhd,kd->hqk", d_mixed_blk, values_here, preferred_element_type=jnp.float32
        )
        delta_row = jnp.sum(soft_probs * d_probs, axis=-1, keepdims=True)
        d_raw = (soft_probs * (d_probs - delta_row) * score_scale).astype(jnp.bfloat16)
        d_query = jnp.einsum(
            "hqk,kd->qhd", d_raw, keys_here, preferred_element_type=jnp.float32
        ).astype(jnp.bfloat16)
        d_keys = d_keys + jnp.einsum(
            "hqk,qhd->kd", d_raw, query_blk, preferred_element_type=jnp.float32
        )
        d_values = d_values + jnp.einsum(
            "hqk,qhd->kd",
            soft_probs.astype(jnp.bfloat16),
            d_mixed_blk,
            preferred_element_type=jnp.float32,
        )
        return ((d_keys, d_values), d_query)

    zero_pair = jnp.zeros((total_len, head_size), jnp.float32)
    (d_keys, d_values), d_query_blocks = lax.scan(
        backward_block, (zero_pair, zero_pair), (starts, query_blocks, d_mixed_blocks, log_totals)
    )
    d_pair = jnp.concatenate([d_keys, d_values], axis=-1).astype(jnp.bfloat16)[:, None, :]
    d_query_heads = d_query_blocks.reshape(total_len, 1, group_width)
    d_query_tok, d_pair_tok = (
        lax.all_to_all(d_query_heads, "seq", split_axis=0, concat_axis=1, tiled=True),
        lax.all_to_all(d_pair, "seq", split_axis=0, concat_axis=1, tiled=True),
    )
    d_query_rot = d_query_tok.astype(jnp.float32).reshape(local_len, head_count, head_size)
    d_query_lin = (
        rotate_back(d_query_rot, cos_tab, sin_tab)
        .reshape(local_len, head_count * head_size)
        .astype(jnp.bfloat16)
    )
    pair_sum = jnp.sum(
        d_pair_tok.astype(jnp.float32).reshape(local_len, kv_count, copies, 2 * head_size), axis=2
    )
    d_key_lin = (
        rotate_back(pair_sum[..., :head_size], cos_tab, sin_tab)
        .reshape(local_len, kv_count * head_size)
        .astype(jnp.bfloat16)
    )
    d_value_lin = (
        pair_sum[..., head_size:].reshape(local_len, kv_count * head_size).astype(jnp.bfloat16)
    )
    d_normed = (
        jnp.dot(d_query_lin, query_all, preferred_element_type=jnp.float32)
        + jnp.dot(d_key_lin, key_all, preferred_element_type=jnp.float32)
        + jnp.dot(d_value_lin, value_all, preferred_element_type=jnp.float32)
    )
    d_input_part, grad_attn_gain = norm_one_back(d_normed)
    d_input = (d_hidden + d_input_part).astype(jnp.bfloat16)
    grad_output = by_tokens(d_branch, mixed)
    grad_query = by_tokens(d_query_lin, normed_bf)
    grad_key = by_tokens(d_key_lin, normed_bf)
    grad_value = by_tokens(d_value_lin, normed_bf)
    summed_grads = (
        lax.psum_scatter(grad_query, ("seq", "dp"), scatter_dimension=0, tiled=True),
        lax.psum_scatter(grad_key, ("seq", "dp"), scatter_dimension=0, tiled=True),
        lax.psum_scatter(grad_value, ("seq", "dp"), scatter_dimension=0, tiled=True),
        lax.psum_scatter(grad_output, ("seq", "dp"), scatter_dimension=0, tiled=True),
        lax.psum_scatter(grad_attn_gain, ("seq", "dp"), scatter_dimension=0, tiled=True),
        lax.psum_scatter(grad_mlp_gain, ("seq", "dp"), scatter_dimension=0, tiled=True),
    )
    return (
        result[None],
        d_input[None],
        summed_grads[0],
        summed_grads[1],
        summed_grads[2],
        summed_grads[3],
        grad_gate,
        grad_up,
        grad_down,
        summed_grads[4],
        summed_grads[5],
    )


def solution(mesh):
    in_specs = (
        P("dp", "seq", None),
        P("dp", None),
        P(("seq", "dp"), None),
        P(("seq", "dp"), None),
        P(("seq", "dp"), None),
        P(("seq", "dp"), None),
        P("seq", None),
        P("seq", None),
        P("seq", None),
        P(("seq", "dp")),
        P(("seq", "dp")),
        P("dp", "seq", None),
    )
    out_specs = (
        P("dp", "seq", None),
        P("dp", "seq", None),
        P(("seq", "dp"), None),
        P(("seq", "dp"), None),
        P(("seq", "dp"), None),
        P(("seq", "dp"), None),
        P("seq", None),
        P("seq", None),
        P("seq", None),
        P(("seq", "dp")),
        P(("seq", "dp")),
    )
    return jax.shard_map(shards, mesh=mesh, in_specs=in_specs, out_specs=out_specs, check_vma=False)
```

profile of v0, /device:TPU:0, one launch (start us, length us, event | category | flops | bytes accessed | tf_op | source)
XLA Modules:
  0.0 1972.7 jit_solution(9492914155247691176)
XLA Ops:
  11.7 42.0 %all-reduce.5 = (bf16[2048]{0:T(1024)(128)(2,1)S(1)}, bf16[2048]{0:T(1024)(128)(2,1)S(1)}) all-reduce(bf16[2048]{0:T(1024)(128)(2,1)S(1)} %dynamic-update-slice, bf16[2048]{0:T(1024)(128)(2,1)S(1)} %dynamic-update-slice.1), channel_id=1, replica_groups=mesh['seq'=8,'dp'=4] {'seq','dp'}, use_global_device_ids=true, to_apply=%add | all-reduce | flops 4096 | bytes 16384
  56.9 13.2 all-gather.12.cloned.1.call-done
  72.8 55.4 %all-gather.10.cloned.1.call-done = bf16[512,2048]{1,0:T(8,128)(2,1)} async-done(((bf16[16,2048]{1,0:T(8,128)(2,1)}), bf16[512,2048]{1,0:T(8,128)(2,1)}) %all-gather.10.cloned.1.call-update) | async-done | bytes 2097168 | tf_op jit(solution)/shard_map/all_gather | solution.py:112
  134.8 72.3 %all-gather.8.cloned.1.call-done = bf16[2048,2048]{1,0:T(8,128)(2,1)} async-done(((bf16[64,2048]{1,0:T(8,128)(2,1)}), bf16[2048,2048]{1,0:T(8,128)(2,1)}) %all-gather.8.cloned.1.call-update) | async-done | bytes 8388624 | tf_op jit(solution)/shard_map/all_gather | solution.py:111
  218.4 9.9 all-to-all-done
  229.0 20.2 %while.28 = (s32[]{:T(128)}, bf16[2,512,4,64]{1,3,2,0:T(8,128)(2,1)S(1)}, f32[2,4,512]{2,1,0:T(4,128)S(1)}, s32[2]{0:T(128)S(1)}, s32[1024]{0:T(1024)S(1)}, /*in...) while((s32[]{:T(128)}, ...), condition=%wide.region_7.8_spmd.clone, body=%wide.region_4.7_spmd.clone.sunk | while | flops 561641984 | bytes 28129464 | solution.py:164
  259.7 15.2 all-to-all-done.2
  275.8 19.5 all-gather.14.cloned.1.call-done
  303.2 34.9 %all-gather.16.cloned.1.call-done = bf16[1024,2048]{1,0:T(8,128)(2,1)} async-done(((bf16[128,2048]{1,0:T(8,128)(2,1)}), bf16[1024,2048]{1,0:T(8,128)(2,1)}) %all-gather.16.cloned.1.call-update) | async-done | bytes 4194320 | tf_op jit(solution)/shard_map/all_gather | solution.py:172
  338.1 10.1 fusion.143
  354.7 21.7 %all-gather.18.cloned.1.call-done = bf16[1,1024,2048]{2,1,0:T(8,128)(2,1)} async-done(((bf16[1,128,2048]{2,1,0:T(8,128)(2,1)}), bf16[1,1024,2048]{2,1,0:T(8,128)(2,1)}) %all-gather.18.cloned.1.call-update) | async-done | bytes 4194320 | tf_op jit(solution)/shard_map/all_gather | solution.py:183
  376.5 13.4 multiply_convert_fusion
  400.8 9.3 convolution_convert_fusion.2
  410.2 10.2 convolution_convert_fusion.1
  433.0 18.8 reduce-scatter.9.cloned.1.call-done
  453.2 53.7 %reduce-scatter.7.cloned.1.call-done = bf16[128,2048]{1,0:T(8,128)(2,1)} async-done(((bf16[1024,2048]{1,0:T(8,128)(2,1)}), bf16[128,2048]{1,0:T(8,128)(2,1)}) %reduce-scatter.7.cloned.1.call-update) | async-done | bytes 524304 | tf_op jit(solution)/shard_map/reduce_scatter | solution.py:177
  518.8 9.4 all-to-all-done.3
  528.8 109.0 %while.29 = (s32[]{:T(128)}, f32[1024,64]{0,1:T(8,128)}, f32[1024,64]{0,1:T(8,128)}, bf16[2,512,4,64]{1,3,2,0:T(8,128)(2,1)S(1)}, s32[2]{0:T(128)S(1)}, /*index=...) while((s32[]{:T(128)}, f32[1024,64]{0,1:T(8,128)}, ...), condition=%wide.region_14.15_spmd.clone, body=%wide.region_12.14_spmd.clone.sunk | while | flops 1398675968 | bytes 98244832 | solution.py:242
  541.9 18.3 fusion.214
  565.7 17.3 fusion.216
  596.1 18.5 fusion.214
  620.1 17.7 fusion.216
  640.1 9.7 all_to_all.81
  656.2 8.1 fusion.129
  673.7 12.3 all_to_all.82
  690.6 8.2 fusion.118
  707.3 42.4 %all-reduce.4 = (f32[2048]{0:T(1024)S(1)}, f32[2048]{0:T(1024)S(1)}) all-reduce(f32[2048]{0:T(1024)S(1)} %get-tuple-element.281, f32[2048]{0:T(1024)S(1)} %get-tuple-element.279), channel_id=9, replica_groups=mesh['seq'=8,'dp'=4] {'seq','dp'}, use_global_device_ids=true, to_apply=%region_24.25.clone | all-reduce | flops 4096 | bytes 32768
  752.0 184.8 %all-reduce.9.cloned.1.call-done = (bf16[1024,2048]{1,0:T(8,128)(2,1)}, bf16[1024,2048]{1,0:T(8,128)(2,1)}, bf16[1024,2048]{1,0:T(8,128)(2,1)}) async-done(((bf16[1024,2048]{1,0:T(8,128)(2,1)}, bf16[1024,2048]{1,0:T(8,128)(2,1)}, bf16[1024,2048]{1,0:T(8,128)(2,1)}), (bf16[1024,2048]{1,0:T(8,128)(2,1)}, bf16[1024,2048]{1,0:T(8,128)(2,1)}, bf16[1024,2048]{1,0:T(8,128)(2,1)})) %all-reduce.9.cloned.1.call-update) | async-done | bytes 12582928 | tf_op jit(solution)/shard_map/psum | solution.py:199
  952.5 135.4 %reduce-scatter.13.cloned.1.call-done = f32[16,2048]{1,0:T(8,128)} async-done(((f32[512,2048]{1,0:T(8,128)}), f32[16,2048]{1,0:T(8,128)}) %reduce-scatter.13.cloned.1.call-update) | async-done | bytes 131088 | tf_op jit(solution)/shard_map/reduce_scatter | solution.py:281
  1087.9 151.2 %reduce-scatter.15.cloned.1.call-done = f32[16,2048]{1,0:T(8,128)} async-done(((f32[512,2048]{1,0:T(8,128)}), f32[16,2048]{1,0:T(8,128)}) %reduce-scatter.15.cloned.1.call-update) | async-done | bytes 131088 | tf_op jit(solution)/shard_map/reduce_scatter | solution.py:282
  1239.1 362.0 %reduce-scatter.17.cloned.1.call-done = f32[64,2048]{1,0:T(8,128)} async-done(((f32[2048,2048]{1,0:T(8,128)}), f32[64,2048]{1,0:T(8,128)}) %reduce-scatter.17.cloned.1.call-update) | async-done | bytes 524304 | tf_op jit(solution)/shard_map/reduce_scatter | solution.py:283
  1601.1 364.8 %reduce-scatter.11.cloned.1.call-done = f32[64,2048]{1,0:T(8,128)} async-done(((f32[2048,2048]{1,0:T(8,128)}), f32[64,2048]{1,0:T(8,128)}) %reduce-scatter.11.cloned.1.call-update) | async-done | bytes 524304 | tf_op jit(solution)/shard_map/reduce_scatter | solution.py:280
  (218 shorter events, 190.0 us)
Async XLA Ops:
  7.2 121.0 %copy-start = (bf16[1,128,2048]{2,1,0:T(8,128)(2,1)S(1)}, bf16[1,128,2048]{2,1,0:T(8,128)(2,1)}, u32[]{:S(2)}) copy-start(bf16[1,128,2048]{2,1,0:T(8,128)(2,1)} %param.16) | copy-start | bytes 1572868
  7.2 62.9 %all-gather.12.cloned.1.call-start = ((), (), s32[]{:S(2)}) async-start(), calls=%async_computation.14 | async-start | bytes 2162688 | tf_op jit(solution)/shard_map/all_gather | solution.py:113
  7.9 120.3 %all-gather.10.cloned.1.call-start = ((), (), s32[]{:S(2)}) async-start(), calls=%async_computation.13 | async-start | bytes 2162688 | tf_op jit(solution)/shard_map/all_gather | solution.py:112
  8.7 198.4 %all-gather.8.cloned.1.call-start = ((), (), s32[]{:S(2)}) async-start(), calls=%async_computation.12 | async-start | bytes 8650752 | tf_op jit(solution)/shard_map/all_gather | solution.py:111
  9.4 285.9 %all-gather.14.cloned.1.call-start = ((), (), s32[]{:S(2)}) async-start(), calls=%async_computation.15 | async-start | bytes 8650752 | tf_op jit(solution)/shard_map/all_gather | solution.py:114
  53.7 153.4 %copy-start.13 = (f32[2048]{0:T(1024)}, f32[2048]{0:T(1024)S(1)}, u32[]{:S(2)}) copy-start(f32[2048]{0:T(1024)S(1)} %convert_element_type.205) | copy-start | bytes 24580
  55.6 157.5 %copy-start.9 = (f32[128,64]{0,1:T(8,128)}, f32[128,64]{0,1:T(8,128)S(1)}, u32[]{:S(2)}) copy-start(f32[128,64]{0,1:T(8,128)S(1)} %get-tuple-element.351) | copy-start | bytes 98308
  55.6 157.5 %copy-start.11 = (f32[128,64]{0,1:T(8,128)}, f32[128,64]{0,1:T(8,128)S(1)}, u32[]{:S(2)}) copy-start(f32[128,64]{0,1:T(8,128)S(1)} %get-tuple-element.352) | copy-start | bytes 98308
  56.9 156.1 %copy-start.17 = (f32[128]{0:T(128)}, f32[128]{0:T(128)S(1)}, u32[]{:S(2)}) copy-start(f32[128]{0:T(128)S(1)} %fusion.101) | copy-start | bytes 1540
  56.9 156.1 %copy-start.15 = (f32[128]{0:T(128)}, f32[128]{0:T(128)S(1)}, u32[]{:S(2)}) copy-start(f32[128]{0:T(128)S(1)} %fusion.134) | copy-start | bytes 1540
  131.4 82.7 %all-to-all-start.1 = ((bf16[128,8,128]{0,2,1:T(8,128)(2,1)}), bf16[128,8,128]{0,2,1:T(8,128)(2,1)S(1)}, u32[]{:S(2)}, u32[]{:S(2)}) async-start(bf16[128,8,128]{0,2,1:T(8,128)(2,1)} %pad_maximum_fusion.1), calls=%async_computation.1 | async-start | bytes 524288 | tf_op jit(solution)/shard_map/all_to_all | solution.py:134
  214.1 14.2 all-to-all-start
  255.9 19.0 all-to-all-start.2
  259.4 78.8 %all-gather.16.cloned.1.call-start = ((), (), s32[]{:S(2)}) async-start(), calls=%async_computation.16 | async-start | bytes 4718592 | tf_op jit(solution)/shard_map/all_gather | solution.py:172
  275.8 25.8 %copy-start.3 = (bf16[128,8,1,256]{0,3,1,2:T(8,128)(2,1)}, bf16[128,8,1,256]{0,3,1,2:T(8,128)(2,1)S(1)}, u32[]{:S(2)}) copy-start(bf16[128,8,1,256]{0,3,1,2:T(8,128)(2,1)S(1)} %copy.120) | copy-start | bytes 1572868
  302.6 73.9 %all-gather.18.cloned.1.call-start = ((), (), s32[]{:S(2)}) async-start(), calls=%async_computation.23 | async-start | bytes 4718592 | tf_op jit(solution)/shard_map/all_gather | solution.py:183
  303.2 148.7 %reduce-scatter.9.cloned.1.call-start = ((), (), s32[]{:S(2)}) async-start(), calls=%async_computation.18 | async-start | bytes 4718592 | tf_op jit(solution)/shard_map/reduce_scatter | solution.py:189
  376.5 13.4 copy-start.19
  400.5 106.4 %reduce-scatter.7.cloned.1.call-start = ((), (), s32[]{:S(2)}) async-start(), calls=%async_computation.17 | async-start | bytes 4718592 | tf_op jit(solution)/shard_map/reduce_scatter | solution.py:177
  410.1 526.7 %all-reduce.9.cloned.1.call-start = ((), (), s32[]{:S(2)}) async-start(), calls=%async_computation.24 | async-start | bytes 25165824 | tf_op jit(solution)/shard_map/psum | solution.py:199
  433.0 74.0 %copy-start.7 = (bf16[1,128,2048]{2,1,0:T(8,128)(2,1)S(1)}, bf16[1,128,2048]{2,1,0:T(8,128)(2,1)}, u32[]{:S(2)}) copy-start(bf16[1,128,2048]{2,1,0:T(8,128)(2,1)} %param.27) | copy-start | bytes 1572868
  515.0 13.2 all-to-all-start.3
  518.5 569.4 %reduce-scatter.13.cloned.1.call-start = ((), (), s32[]{:S(2)}) async-start(), calls=%async_computation.20 | async-start | bytes 4325376 | tf_op jit(solution)/shard_map/reduce_scatter | solution.py:281
  637.8 12.4 copy-start.12
  637.8 12.5 copy-start.10
  637.8 12.5 copy-start.1
  637.8 12.5 copy-start.14
  637.9 12.5 copy-start.16
  653.2 585.9 %reduce-scatter.15.cloned.1.call-start = ((), (), s32[]{:S(2)}) async-start(), calls=%async_computation.21 | async-start | bytes 4325376 | tf_op jit(solution)/shard_map/reduce_scatter | solution.py:282
  656.1 945.0 %reduce-scatter.17.cloned.1.call-start = ((), (), s32[]{:S(2)}) async-start(), calls=%async_computation.22 | async-start | bytes 17301504 | tf_op jit(solution)/shard_map/reduce_scatter | solution.py:283
  664.3 1301.7 %reduce-scatter.11.cloned.1.call-start = ((), (), s32[]{:S(2)}) async-start(), calls=%async_computation.19 | async-start | bytes 17301504 | tf_op jit(solution)/shard_map/reduce_scatter | solution.py:280
  705.0 45.9 %copy-start.18 = (f32[128]{0:T(128)S(1)}, f32[128]{0:T(128)}, u32[]{:S(2)}) copy-start(f32[128]{0:T(128)} %copy-done.17) | copy-start | bytes 1540
  (14 other events, 87.6 us)
Sparse Core Ops, SparseCore 0:
  10.9 59.0 all-gather.11
  73.0 55.2 all-gather.9
  131.2 75.9 all-gather.7
  209.9 85.3 all-gather.13
  302.7 35.3 all-gather.15
  339.9 36.5 all-gather.17
  400.7 51.1 reduce-scatter.8
  455.8 51.1 reduce-scatter.6
  510.3 426.3 all-reduce.8
  939.5 148.3 reduce-scatter.12
  1090.8 148.3 reduce-scatter.14
  1241.9 359.2 reduce-scatter.16
  1604.0 361.9 reduce-scatter.10
where the time goes:
time: 1980 us; the launch traced here: 1970 us
  waiting for transfers between devices  1530 us (77%)
  matrix products  232 us (12%)
  blocking collectives  106 us (5%)
  other arithmetic  49.3 us (2%)
  local copies, waits for them, and re-layouts  21.7 us (1%)
    reduce_scatter x1, waiting for transfers between devices, shards(): lax.psum_scatter(grad_query, ('seq', 'dp'), scatter_dimension=0, tiled=True)  365 us
    reduce_scatter x1, waiting for transfers between devices, shards(): lax.psum_scatter(grad_output, ('seq', 'dp'), scatter_dimension=0, tiled=T...  362 us
    psum x1, waiting for transfers between devices, shards(): lax.psum(grad_gate.astype(jnp.bfloat16), 'dp').astype(jnp.float32)  185 us
    reduce_scatter x1, waiting for transfers between devices, shards(): lax.psum_scatter(grad_value, ('seq', 'dp'), scatter_dimension=0, tiled=True)  151 us
    reduce_scatter x1, waiting for transfers between devices, shards(): lax.psum_scatter(grad_key, ('seq', 'dp'), scatter_dimension=0, tiled=True)  135 us
    unnamed x2, blocking collectives  84.4 us
    all_gather x1, waiting for transfers between devices, shards(): lax.all_gather(query_weight, ('seq', 'dp'), axis=0, tiled=True)  72.3 us
    all_gather x1, waiting for transfers between devices, shards(): lax.all_gather(key_weight, ('seq', 'dp'), axis=0, tiled=True)  55.4 us
  transfers between devices with their start and end apart: 17, of which 16 were waited for; matrix products, arithmetic and copies ran while one was open for 14% of the time, Pallas kernels for 0%

commit v1 on v0

v1 whole, which is shorter than its diff:
```python
import functools
import math

import jax
import jax.numpy as jnp
from jax import lax
from jax.experimental import pallas as pl
from jax.experimental.pallas import tpu as pltpu
from jax.sharding import PartitionSpec as P

HEADS = 32
KV_HEADS = 8
HEAD_DIM = 64
HALF = HEAD_DIM // 2
NEG = -1e30

norm_eps = 1e-05
bf16 = jnp.bfloat16
f32 = jnp.float32


def by_rows(left, weight_mat):
    return lax.dot_general(
        left, weight_mat, (((1,), (1,)), ((), ())), preferred_element_type=f32
    )


def by_tokens(left, right):
    return lax.dot_general(
        left, right, (((0,), (0,)), ((), ())), preferred_element_type=f32
    )


def plain(left, right):
    return jnp.dot(left, right, preferred_element_type=f32)


def rms_norm(values, gain_vec):
    return (
        values * lax.rsqrt(jnp.mean(values * values, axis=-1, keepdims=True) + norm_eps) * gain_vec
    )


def rope_tables(positions):
    exponent = jnp.arange(HALF, dtype=f32) * 2.0 / HEAD_DIM
    inverse = 1.0 / 500000.0**exponent
    wavelen = 2.0 * math.pi / inverse
    scaled = jnp.where(wavelen > 8192.0, inverse / 32.0, inverse)
    smooth = (8192.0 / wavelen - 1.0) / 3.0
    smoothed = (1.0 - smooth) * scaled / 32.0 + smooth * scaled
    medium = (wavelen >= 2048.0) & (wavelen <= 8192.0)
    inverse = jnp.where(medium, smoothed, scaled)
    angles = positions.astype(f32)[:, None] * inverse[None, :]
    return (jnp.cos(angles), jnp.sin(angles))


def turn(first, second, cos_tab, sin_tab):
    return (first * cos_tab - second * sin_tab, second * cos_tab + first * sin_tab)


def turn_back(first, second, cos_tab, sin_tab):
    return (first * cos_tab + second * sin_tab, second * cos_tab - first * sin_tab)


def gate_grads(d_active, gate_val, up_val, sigmoid_val):
    d_gate = (d_active * up_val * sigmoid_val * (1.0 + gate_val * (1.0 - sigmoid_val))).astype(bf16)
    d_up = (d_active * gate_val * sigmoid_val).astype(bf16)
    return (d_gate, d_up)


def hops(index, count):
    if count == 8:
        return (2, 4) if index % 2 == 0 else (4, 2)
    return tuple(1 << bit for bit in range(1, count.bit_length() - 1))


def half_order(index, count):
    blocks = [index]
    for hop in hops(index, count):
        blocks = blocks + [block ^ hop for block in blocks]
    return blocks


def order_of(index, count):
    return half_order(index, count) + half_order(index ^ 1, count)


def swap(values, count, stage):
    if stage < 0:
        perm = [(i, i ^ 1) for i in range(count)]
    else:
        perm = [(i, i ^ hops(i, count)[stage]) for i in range(count)]
    return lax.ppermute(values, "seq", perm)


def gather_blocks(values, count):
    held = values[None]
    pieces = [values[None]]
    others = []
    for stage in range(len(hops(0, count))):
        arrived = swap(held, count, stage)
        if stage > 0 or len(hops(0, count)) == 1:
            others.append(swap(held if stage == 1 else pieces[-1], count, -1))
        pieces.append(arrived)
        held = jnp.concatenate([held, arrived], axis=0)
    others.append(swap(pieces[-1], count, -1))
    return jnp.concatenate(pieces + others, axis=0)


def scatter_blocks(blocks, count):
    half = count // 2
    total = blocks[:half].astype(f32) + swap(blocks[half:], count, -1).astype(f32)
    for stage in reversed(range(len(hops(0, count)))):
        half = half // 2
        arrived = swap(total[half:].astype(bf16), count, stage)
        total = total[:half] + arrived.astype(f32)
    return total[0]


def ring_gather(values, count):
    pieces = [values]
    for _ in range(count - 1):
        pieces.append(
            lax.ppermute(pieces[-1], "dp", [(i, (i + 1) % count) for i in range(count)])
        )
    return pieces


def in_order(pieces, count):
    stacked = jnp.stack(pieces)
    here = lax.axis_index("dp")
    return jnp.concatenate(
        [
            lax.dynamic_slice_in_dim(stacked, lax.rem(here - i + count, count), 1, 0)
            for i in range(count)
        ]
    )


def ring_scatter(blocks, count):
    here = lax.axis_index("dp")

    def mine(step):
        return lax.dynamic_index_in_dim(
            blocks, lax.rem(here - 1 - step + count, count), 0, keepdims=False
        )

    total = mine(0)
    for step in range(1, count):
        arrived = lax.ppermute(
            total.astype(bf16), "dp", [(i, (i + 1) % count) for i in range(count)]
        )
        total = arrived.astype(f32) + mine(step)
    return total


def sum_everywhere(values, seq_count, dp_count):
    bit = 1
    while bit < dp_count:
        values = values + lax.ppermute(values, "dp", [(i, i ^ bit) for i in range(dp_count)])
        bit *= 2
    bit = 1
    while bit < seq_count:
        values = values + lax.ppermute(values, "seq", [(i, i ^ bit) for i in range(seq_count)])
        bit *= 2
    return values


def picker(width, head, halves):
    lane = lax.broadcasted_iota(jnp.int32, (width, HEAD_DIM), 0)
    part = lax.broadcasted_iota(jnp.int32, (width, HEAD_DIM), 1)
    if halves:
        target = (part // HALF) * (width // 2) + head * HALF + part % HALF
    else:
        target = head * HEAD_DIM + part
    return jnp.where(lane == target, 1.0, 0.0).astype(bf16)


def tile_bias(ends_ref, docs, row_begin, rows, key_begin, keys):
    row = row_begin + lax.broadcasted_iota(jnp.int32, (rows, 1), 0)
    doc_begin = jnp.zeros((rows, 1), jnp.int32)
    for j in range(docs):
        doc_begin = jnp.maximum(doc_begin, jnp.where(row >= ends_ref[j], ends_ref[j], 0))
    key = key_begin + lax.broadcasted_iota(jnp.int32, (rows, keys), 1)
    return jnp.where((key >= doc_begin) & (key <= row), 0.0, NEG)


def row_blocks(total_len):
    rows = min(256, total_len)
    window = total_len // 2
    spans = []
    for begin in range(0, total_len, rows):
        low = max(0, (begin - window + 1) // rows * rows)
        spans.append((begin, low, begin + rows - low))
    return rows, spans


def contract_first(left, right):
    return lax.dot_general(left, right, (((0,), (0,)), ((), ())), preferred_element_type=f32)


def forward_kernel(place_ref, ends_ref, q_ref, k_ref, v_ref, o_ref, log_ref, qs, ks, vs, bias, acc, *, docs, blocks):
    total_len, width = q_ref.shape
    local = total_len // blocks
    for b in range(blocks):
        source = pl.ds(pl.multiple_of(place_ref[b] * local, local), local)
        target = pl.ds(b * local, local)
        qs[target, :] = q_ref[source, :]
        ks[target, :] = k_ref[source, :]
        vs[target, :] = v_ref[source, :]
    rows, spans = row_blocks(total_len)
    for begin, low, keys in spans:
        bias[:, :keys] = tile_bias(ends_ref, docs, begin, rows, low, keys)
        acc[...] = jnp.zeros_like(acc)

        @pl.loop(0, width // HEAD_DIM)
        def _(head):
            q_head = plain(qs[begin : begin + rows, :], picker(width, head, True)).astype(bf16)
            scores = by_rows(q_head, ks[low : low + keys, :]) + bias[:, :keys]
            peak = jnp.max(scores, axis=-1, keepdims=True)
            probs = jnp.exp(scores - peak)
            total = jnp.sum(probs, axis=-1, keepdims=True)
            mixed = plain(probs.astype(bf16), vs[low : low + keys, :]) / total
            acc[...] += by_rows(mixed.astype(bf16), picker(width, head, False))
            log_ref[head, begin : begin + rows, :] = jnp.broadcast_to(
                peak + jnp.log(total), (rows, 128)
            )

        o_ref[begin : begin + rows, :] = acc[...].astype(bf16)


def backward_kernel(
    place_ref, ends_ref, q_ref, k_ref, v_ref, g_ref, log_ref, dq_ref, dk_ref, dv_ref,
    qs, ks, vs, bias, acc, dq, dk, dv, *, docs, blocks,
):
    total_len, width = q_ref.shape
    local = total_len // blocks
    for b in range(blocks):
        source = pl.ds(pl.multiple_of(place_ref[b] * local, local), local)
        target = pl.ds(b * local, local)
        qs[target, :] = q_ref[source, :]
        ks[target, :] = k_ref[source, :]
        vs[target, :] = v_ref[source, :]
    rows, spans = row_blocks(total_len)
    dk[...] = jnp.zeros_like(dk)
    dv[...] = jnp.zeros_like(dv)
    for begin, low, keys in spans:
        bias[:, :keys] = tile_bias(ends_ref, docs, begin, rows, low, keys)
        acc[...] = jnp.zeros_like(acc)

        @pl.loop(0, width // HEAD_DIM)
        def _(head):
            q_pick = picker(width, head, True)
            q_head = plain(qs[begin : begin + rows, :], q_pick).astype(bf16)
            g_head = plain(g_ref[begin : begin + rows, :], picker(width, head, False)).astype(bf16)
            keys_here = ks[low : low + keys, :]
            scores = by_rows(q_head, keys_here) + bias[:, :keys]
            probs = jnp.exp(scores - log_ref[head, begin : begin + rows, 0:1])
            d_probs = by_rows(g_head, vs[low : low + keys, :])
            pushed = probs * d_probs
            delta = jnp.sum(pushed, axis=-1, keepdims=True)
            d_raw = (pushed - probs * delta).astype(bf16)
            d_query = plain(d_raw, keys_here) * (HEAD_DIM ** (-0.5))
            acc[...] += by_rows(d_query.astype(bf16), q_pick)
            dk[low : low + keys, :] += contract_first(d_raw, q_head)
            dv[low : low + keys, :] += contract_first(probs.astype(bf16), g_head)

        dq[begin : begin + rows, :] = acc[...].astype(bf16)
    for b in range(blocks):
        source = pl.ds(b * local, local)
        target = pl.ds(pl.multiple_of(place_ref[b] * local, local), local)
        dq_ref[target, :] = dq[source, :]
        dk_ref[target, :] = dk[source, :].astype(bf16)
        dv_ref[target, :] = dv[source, :].astype(bf16)


def smem():
    return pl.BlockSpec(memory_space=pltpu.SMEM)


def vmem():
    return pl.BlockSpec(memory_space=pltpu.VMEM)


def attend(place, ends, query, key, value, blocks):
    total_len, width = query.shape
    heads = width // HEAD_DIM
    rows, spans = row_blocks(total_len)
    most = max(keys for _, _, keys in spans)
    return pl.pallas_call(
        functools.partial(forward_kernel, docs=ends.shape[0], blocks=blocks),
        out_shape=(
            jax.ShapeDtypeStruct((total_len, width), bf16),
            jax.ShapeDtypeStruct((heads, total_len, 128), f32),
        ),
        in_specs=[smem(), smem(), vmem(), vmem(), vmem()],
        out_specs=(vmem(), vmem()),
        scratch_shapes=[
            pltpu.VMEM((total_len, width), bf16),
            pltpu.VMEM((total_len, HEAD_DIM), bf16),
            pltpu.VMEM((total_len, HEAD_DIM), bf16),
            pltpu.VMEM((rows, most), f32),
            pltpu.VMEM((rows, width), f32),
        ],
        cost_estimate=pl.CostEstimate(
            flops=4 * heads * total_len * total_len * HEAD_DIM,
            bytes_accessed=4 * total_len * width * 2,
            transcendentals=heads * total_len * total_len,
        ),
    )(place, ends, query, key, value)


def attend_back(place, ends, query, key, value, grad, logs, blocks):
    total_len, width = query.shape
    heads = width // HEAD_DIM
    rows, spans = row_blocks(total_len)
    most = max(keys for _, _, keys in spans)
    return pl.pallas_call(
        functools.partial(backward_kernel, docs=ends.shape[0], blocks=blocks),
        out_shape=(
            jax.ShapeDtypeStruct((total_len, width), bf16),
            jax.ShapeDtypeStruct((total_len, HEAD_DIM), bf16),
            jax.ShapeDtypeStruct((total_len, HEAD_DIM), bf16),
        ),
        in_specs=[smem(), smem(), vmem(), vmem(), vmem(), vmem(), vmem()],
        out_specs=(vmem(), vmem(), vmem()),
        scratch_shapes=[
            pltpu.VMEM((total_len, width), bf16),
            pltpu.VMEM((total_len, HEAD_DIM), bf16),
            pltpu.VMEM((total_len, HEAD_DIM), bf16),
            pltpu.VMEM((rows, most), f32),
            pltpu.VMEM((rows, width), f32),
            pltpu.VMEM((total_len, width), bf16),
            pltpu.VMEM((total_len, HEAD_DIM), f32),
            pltpu.VMEM((total_len, HEAD_DIM), f32),
        ],
        cost_estimate=pl.CostEstimate(
            flops=10 * heads * total_len * total_len * HEAD_DIM,
            bytes_accessed=8 * total_len * width * 2,
            transcendentals=heads * total_len * total_len,
        ),
    )(place, ends, query, key, value, grad, logs)


def shards(
    tokens,
    doc_lengths,
    query_weight,
    key_weight,
    value_weight,
    output_weight,
    gate_weight,
    up_weight,
    down_weight,
    attn_gain,
    mlp_gain,
    cotangent,
):
    groups = lax.axis_size("seq")
    dp_count = lax.axis_size("dp")
    my_index = lax.axis_index("seq")
    my_seq = lax.axis_index("dp")
    local_len, width = tokens.shape[1:]
    total_len = local_len * groups
    per_group = HEADS // groups
    copies = groups // KV_HEADS
    group_width = per_group * HEAD_DIM
    gain_rows = attn_gain.shape[0]
    kv_rows = HEAD_DIM // copies
    share = (dp_count - 1) * total_len <= 3 * gate_weight.shape[0]
    my_place = my_index * dp_count + my_seq

    order = jnp.asarray([order_of(i, groups) for i in range(groups)], jnp.int32)[my_index]
    place = jnp.asarray(
        [[order_of(i, groups).index(b) for b in range(groups)] for i in range(groups)], jnp.int32
    )[my_index]

    inputs = tokens[0].astype(f32)
    cot_bf = cotangent[0]

    gains_here = jnp.stack([attn_gain, mlp_gain])
    gains = sum_everywhere(
        lax.dynamic_update_slice(
            jnp.zeros((2, width), bf16), gains_here, (0, my_place * gain_rows)
        ),
        groups,
        dp_count,
    ).astype(f32)
    attn_gain_all, mlp_gain_all = gains[0], gains[1]

    tokens_all = gather_blocks(tokens[0], groups).reshape(total_len, width)
    rows_here = jnp.concatenate([query_weight, key_weight, value_weight], axis=0)
    rows_all = in_order(ring_gather(rows_here, dp_count), dp_count)
    q_rows = query_weight.shape[0]
    k_rows = key_weight.shape[0]
    query_rows = (
        rows_all[:, :q_rows]
        .reshape(per_group, 2, HALF, width)
        .transpose(1, 0, 2, 3)
        .reshape(group_width, width)
    )
    pair_rows = jnp.stack(
        [
            rows_all[:, q_rows : q_rows + k_rows].reshape(kv_rows, width),
            rows_all[:, q_rows + k_rows :].reshape(kv_rows, width),
        ]
    )
    pair_parts = [pair_rows]
    for _ in range(copies.bit_length() - 1):
        step = len(pair_parts)
        arrived = [
            lax.ppermute(part, "seq", [(i, i ^ step) for i in range(groups)]) for part in pair_parts
        ]
        pair_parts = pair_parts + arrived
    if copies > 1:
        stacked = jnp.stack(pair_parts)
        copy_index = lax.rem(my_index, copies)
        pair_rows = jnp.concatenate(
            [
                lax.dynamic_index_in_dim(
                    stacked, jnp.bitwise_xor(copy_index, i), 0, keepdims=False
                )
                for i in range(copies)
            ],
            axis=1,
        )
    key_rows, value_rows = pair_rows[0], pair_rows[1]
    lin_rows = jnp.concatenate([query_rows, key_rows, value_rows], axis=0)

    inputs_all = tokens_all.astype(f32)
    scale_all = lax.rsqrt(jnp.mean(inputs_all * inputs_all, axis=-1, keepdims=True) + norm_eps)
    normed_all = (inputs_all * scale_all * attn_gain_all).astype(bf16)
    lin = by_rows(normed_all, lin_rows)

    ends = jnp.cumsum(doc_lengths[0], dtype=jnp.int32)
    places = (order[:, None] * local_len + jnp.arange(local_len, dtype=jnp.int32)[None]).reshape(-1)
    begins = jnp.max(jnp.where(places[:, None] >= ends[None, :], ends[None, :], 0), axis=1)
    cos_tab, sin_tab = rope_tables(places - begins)
    cos_wide, sin_wide = jnp.tile(cos_tab, (1, per_group)), jnp.tile(sin_tab, (1, per_group))
    half_width = group_width // 2
    score_scale = HEAD_DIM ** (-0.5)
    query = jnp.concatenate(
        turn(lin[:, :half_width], lin[:, half_width:group_width], cos_wide, sin_wide), axis=1
    ).astype(bf16) * jnp.asarray(score_scale, bf16)
    key = jnp.concatenate(
        turn(
            lin[:, group_width : group_width + HALF],
            lin[:, group_width + HALF : group_width + HEAD_DIM],
            cos_tab,
            sin_tab,
        ),
        axis=1,
    ).astype(bf16)
    value = lin[:, group_width + HEAD_DIM :].astype(bf16)

    mixed_heads, logs = attend(place, ends, query, key, value, groups)
    mixed = lax.all_to_all(
        mixed_heads.reshape(groups, local_len, group_width),
        "seq",
        split_axis=0,
        concat_axis=0,
        tiled=True,
    )
    mixed = mixed.transpose(1, 0, 2).reshape(local_len, groups * group_width)

    output_rows = in_order(ring_gather(output_weight, dp_count), dp_count).reshape(-1, HEADS * HEAD_DIM)
    block_width = output_rows.shape[0]
    output_all = gather_blocks(output_rows, groups).reshape(width, HEADS * HEAD_DIM)

    def features_in_order(values):
        return jnp.concatenate(
            [
                lax.dynamic_slice_in_dim(values, place[b] * block_width, block_width, 1)
                for b in range(groups)
            ],
            axis=1,
        )

    def features_by_order(values):
        return jnp.concatenate(
            [
                lax.dynamic_slice_in_dim(values, order[b] * block_width, block_width, 1)
                for b in range(groups)
            ],
            axis=1,
        )

    hidden_state = inputs + features_in_order(by_rows(mixed, output_all))
    normed_two, norm_two_back = jax.vjp(rms_norm, hidden_state, mlp_gain_all)
    normed_two_bf = normed_two.astype(bf16)

    def forward_mlp(normed_toks, cot_toks):
        gate_val = by_rows(normed_toks, gate_weight)
        up_val = by_rows(normed_toks, up_weight)
        sigmoid_val = 1.0 / (1.0 + jnp.exp(-gate_val))
        active = (gate_val * sigmoid_val * up_val).astype(bf16)
        d_active = by_rows(cot_toks, down_weight)
        d_gate, d_up = gate_grads(d_active, gate_val, up_val, sigmoid_val)
        return active, d_gate, d_up

    cot_all = gather_blocks(cot_bf, groups).reshape(total_len, width)
    normed_two_all = gather_blocks(normed_two_bf, groups).reshape(total_len, width)
    active, d_gate, d_up = forward_mlp(normed_two_all, cot_all)
    d_normed_two = scatter_blocks(
        (plain(d_gate, gate_weight) + plain(d_up, up_weight))
        .astype(bf16)
        .reshape(groups, local_len, width),
        groups,
    )
    mlp_out = scatter_blocks(
        plain(active, down_weight).astype(bf16).reshape(groups, local_len, width), groups
    )
    result = (hidden_state + mlp_out).astype(bf16)

    d_hidden_part, grad_mlp_gain = norm_two_back(d_normed_two)
    d_hidden = cot_bf.astype(f32) + d_hidden_part
    d_branch = d_hidden.astype(bf16)
    d_mixed = plain(features_by_order(d_branch), output_all).astype(bf16)
    d_mixed_heads = lax.all_to_all(
        d_mixed.reshape(local_len, groups, group_width).transpose(1, 0, 2),
        "seq",
        split_axis=0,
        concat_axis=0,
        tiled=True,
    ).reshape(total_len, group_width)

    grad_gate = by_tokens(d_gate, normed_two_all)
    grad_up = by_tokens(d_up, normed_two_all)
    grad_down = by_tokens(active, cot_all)
    if share:
        far_cot = jnp.concatenate(ring_gather(cot_bf, dp_count)[1:], axis=0)
        far_normed = jnp.concatenate(ring_gather(normed_two_bf, dp_count)[1:], axis=0)
        far_cot = gather_blocks(far_cot, groups).reshape(-1, width)
        far_normed = gather_blocks(far_normed, groups).reshape(-1, width)
        far_active, far_gate, far_up = forward_mlp(far_normed, far_cot)
        grad_gate = grad_gate + by_tokens(far_gate, far_normed)
        grad_up = grad_up + by_tokens(far_up, far_normed)
        grad_down = grad_down + by_tokens(far_active, far_cot)
    else:
        grad_gate, grad_up, grad_down = (
            lax.psum(grad.astype(bf16), "dp").astype(f32) for grad in (grad_gate, grad_up, grad_down)
        )

    mixed_all = gather_blocks(mixed, groups).reshape(total_len, HEADS * HEAD_DIM)
    d_branch_cols = lax.all_to_all(
        d_branch.reshape(local_len, groups, block_width).transpose(1, 0, 2),
        "seq",
        split_axis=0,
        concat_axis=0,
        tiled=True,
    )
    d_branch_cols = jnp.concatenate(
        [lax.dynamic_slice_in_dim(d_branch_cols, order[b], 1, 0) for b in range(groups)]
    ).reshape(total_len, block_width)
    grad_output = ring_scatter(
        by_tokens(d_branch_cols, mixed_all).reshape(dp_count, -1, HEADS * HEAD_DIM), dp_count
    )

    d_query, d_key, d_value = attend_back(
        place, ends, query, key, value, d_mixed_heads, logs, groups
    )
    if copies > 1:
        d_pair = jnp.stack([d_key, d_value])
        total_pair = d_pair.astype(f32)
        step = 1
        while step < copies:
            total_pair = total_pair + lax.ppermute(
                total_pair, "seq", [(i, i ^ step) for i in range(groups)]
            )
            step *= 2
        d_key, d_value = total_pair[0], total_pair[1]
    d_query, d_key = d_query.astype(f32), d_key.astype(f32)
    d_lin = jnp.concatenate(
        [
            *turn_back(d_query[:, :half_width], d_query[:, half_width:], cos_wide, sin_wide),
            *turn_back(d_key[:, :HALF], d_key[:, HALF:], cos_tab, sin_tab),
            d_value.astype(f32),
        ],
        axis=1,
    ).astype(bf16)
    grad_lin = by_tokens(d_lin, normed_all)
    grad_pair = grad_lin[group_width:].reshape(2, copies, dp_count, -1, width)
    if copies > 1:
        grad_pair = lax.dynamic_index_in_dim(
            grad_pair, lax.rem(my_index, copies), 1, keepdims=True
        )
    grad_rows = jnp.concatenate(
        [
            grad_lin[:group_width]
            .reshape(2, per_group, HALF, width)
            .transpose(1, 0, 2, 3)
            .reshape(dp_count, q_rows, width),
            grad_pair[0, 0],
            grad_pair[1, 0],
        ],
        axis=1,
    )
    grad_rows = ring_scatter(grad_rows, dp_count)

    d_lin_own = d_lin
    if copies > 1:
        lane = jnp.arange(d_lin.shape[1], dtype=jnp.int32)
        keep = (lane < group_width) | (lax.rem(my_index, copies) == 0)
        d_lin_own = jnp.where(keep[None], d_lin, jnp.zeros_like(d_lin))
    d_normed_part = plain(d_lin_own, lin_rows).astype(bf16)
    grad_attn_gain = jnp.sum(d_normed_part.astype(f32) * (inputs_all * scale_all), axis=0)
    d_normed = scatter_blocks(d_normed_part.reshape(groups, local_len, width), groups)
    _, norm_one_back = jax.vjp(lambda v: rms_norm(v, attn_gain_all), inputs)
    d_input = (d_hidden + norm_one_back(d_normed)[0]).astype(bf16)

    gain_grads = sum_everywhere(jnp.stack([grad_attn_gain, grad_mlp_gain]), groups, dp_count)
    gain_grads = lax.dynamic_slice(gain_grads, (0, my_place * gain_rows), (2, gain_rows))

    return (
        result[None],
        d_input[None],
        grad_rows[:q_rows],
        grad_rows[q_rows : q_rows + k_rows],
        grad_rows[q_rows + k_rows :],
        grad_output,
        grad_gate,
        grad_up,
        grad_down,
        gain_grads[0],
        gain_grads[1],
    )


def solution(mesh):
    in_specs = (
        P("dp", "seq", None),
        P("dp", None),
        P(("seq", "dp"), None),
        P(("seq", "dp"), None),
        P(("seq", "dp"), None),
        P(("seq", "dp"), None),
        P("seq", None),
        P("seq", None),
        P("seq", None),
        P(("seq", "dp")),
        P(("seq", "dp")),
        P("dp", "seq", None),
    )
    out_specs = (
        P("dp", "seq", None),
        P("dp", "seq", None),
        P(("seq", "dp"), None),
        P(("seq", "dp"), None),
        P(("seq", "dp"), None),
        P(("seq", "dp"), None),
        P("seq", None),
        P("seq", None),
        P("seq", None),
        P(("seq", "dp")),
        P(("seq", "dp")),
    )
    return jax.shard_map(shards, mesh=mesh, in_specs=in_specs, out_specs=out_specs, check_vma=False)
```

time: 1980 us -> 693 us (0.35)
  waiting for transfers between devices: 1530 us -> 199 us
  blocking collectives: 106 us -> 0 us
  local copies, waits for them, and re-layouts: 21.7 us -> 98.3 us
  starting transfers between devices: 15.2 us -> 59.8 us
  Pallas kernels: 0 us -> 36.4 us
    reduce_scatter x6 -> x0, waiting for transfers between devices: 1090 us -> none  [the longest x1 365 us: shards(): lax.psum_scatter(grad_query, ('seq', 'dp'), scatter_dimension=0, tiled=True)]
    all_gather x6 -> x0, waiting for transfers between devices: 217 us -> none  [the longest x1 72.3 us: shards(): lax.all_gather(query_weight, ('seq', 'dp'), axis=0, tiled=True)]
    ppermute x0 -> x65, waiting for transfers between devices: none -> 194 us  [the longest x12 76.6 us: ring_gather(): lax.ppermute(pieces[-1], 'dp', [(i, (i + 1) % count) for i in range(count)])]
    psum x1 -> x0, waiting for transfers between devices: 185 us -> none  [shards(): lax.psum(grad_gate.astype(jnp.bfloat16), 'dp').astype(jnp.float32)]
    dot_general x21 -> x5, matrix products: 140 us -> 27.4 us  [plain(): return jnp.dot(left, right, preferred_element_type=f32)]
    unnamed x2 -> x0, blocking collectives: 84.4 us -> none
    dot_general x7 -> x8, matrix products: 44.6 us -> 106 us  [by_tokens(): lax.dot_general(left, right, (((0,), (0,)), ((), ())), preferred_element_...]
    unnamed x76 -> x191, local copies, waits for them, and re-layouts: 7.14 us -> 60.1 us
  transfers between devices with their start and end apart: 17 -> 68, of which waited for: 16 -> 27; matrix products, arithmetic and copies ran while one was open for 14% -> 32% of each run, Pallas kernels for 0% -> 5%
where the time goes in v1:
time: 693 us; the launch traced here: 687 us
  matrix products  214 us (31%)
  waiting for transfers between devices  199 us (29%)
  local copies, waits for them, and re-layouts  98.3 us (14%)
  starting transfers between devices  59.8 us (9%)
  other arithmetic  51.9 us (7%)
  Pallas kernels  36.4 us (5%)
  between operations  26.9 us (4%)
    dot_general x8, matrix products, by_tokens(): lax.dot_general(left, right, (((0,), (0,)), ((), ())), preferred_element_...  106 us
    dot_general x8, matrix products, by_rows(): lax.dot_general(left, weight_mat, (((1,), (1,)), ((), ())), preferred_ele...  80.6 us
    ppermute x12, waiting for transfers between devices, ring_gather(): lax.ppermute(pieces[-1], 'dp', [(i, (i + 1) % count) for i in range(count)])  76.6 us
    ppermute x37, waiting for transfers between devices, swap(): return lax.ppermute(values, 'seq', perm)  71.2 us
    unnamed x191, local copies, waits for them, and re-layouts  60.1 us
    dot_general x5, matrix products, plain(): return jnp.dot(left, right, preferred_element_type=f32)  27.4 us
    ppermute x6, waiting for transfers between devices, ring_scatter(): lax.ppermute(total.astype(bf16), 'dp', [(i, (i + 1) % count) for i in ran...  23.5 us
    ppermute x37, starting transfers between devices, swap(): return lax.ppermute(values, 'seq', perm)  23.4 us
  transfers between devices with their start and end apart: 68, of which 27 were waited for; matrix products, arithmetic and copies ran while one was open for 32% of the time, Pallas kernels for 5%

profile of v1, /device:TPU:0, one launch (start us, length us, event | category | flops | bytes accessed | tf_op | source)
XLA Modules:
  0.0 687.1 jit_solution(12199977134856311612)
XLA Ops:
  62.8 18.1 %collective-permute-done.13 = bf16[64,2048]{1,0:T(8,128)(2,1)} collective-permute-done((bf16[64,2048]{1,0:T(8,128)(2,1)S(1)}, bf16[64,2048]{1,0:T(8,128)(2,1)}, u32[]{:S(2)}, u32[]{:S(2)}) %collective-permute-start.13) | collective-permute-done | bytes 262176 | tf_op jit(solution)/shard_map/ppermute | solution.py:124
  85.2 7.5 %collective-permute-done.14 = bf16[64,2048]{1,0:T(8,128)(2,1)S(1)} collective-permute-done((bf16[64,2048]{1,0:T(8,128)(2,1)}, bf16[64,2048]{1,0:T(8,128)(2,1)S(1)}, u32[]{:S(2)}, u32[]{:S(2)}) %collective-permute-start.14) | collective-permute-done | bytes 262176 | tf_op jit(solution)/shard_map/ppermute | solution.py:124
  95.1 14.1 %collective-permute-done.47 = bf16[128,2048]{1,0:T(8,128)(2,1)S(1)} collective-permute-done((bf16[128,2048]{1,0:T(8,128)(2,1)S(1)}, bf16[128,2048]{1,0:T(8,128)(2,1)S(1)}, u32[]{:S(2)}, u32[]{:S(2)}) %collective-permute-start.47) | collective-permute-done | bytes 524320 | tf_op jit(solution)/shard_map/ppermute | solution.py:124
  119.0 8.4 %collective-permute-done.48 = bf16[128,2048]{1,0:T(8,128)(2,1)S(1)} collective-permute-done((bf16[128,2048]{1,0:T(8,128)(2,1)S(1)}, bf16[128,2048]{1,0:T(8,128)(2,1)S(1)}, u32[]{:S(2)}, u32[]{:S(2)}) %collective-permute-start.48) | collective-permute-done | bytes 524320 | tf_op jit(solution)/shard_map/ppermute | solution.py:124
  149.5 15.6 %shard_map.221 = (bf16[1024,256]{1,0:T(8,128)(2,1)}, f32[4,1024,128]{2,1,0:T(8,128)}) custom-call(s32[8]{0:T(128)} %get-tuple-element.100.place_ref, s32[8]{0:T(128)} %bitcast.330, bf16[1024,256]{1,0:T(8,128)(2,1)} %maximum_multiply_fusion.q_ref, bf16[1024,64]{1,0:T(8,128)(2,1)} %pad_maximum_fusion.15.k_ref, bf16[1024,64]{1,0:T(8,128)(2,1)} %slice.357.v_ref), custom_call_target="tpu_custom_call" | custom-call | flops 1073741824 | bytes 2097152 | tf_op jit(solution)/shard_map/pallas_call | solution.py:290
  213.6 11.3 %collective-permute-done.19 = bf16[1,128,2048]{2,1,0:T(8,128)(2,1)S(1)} collective-permute-done((bf16[1,128,2048]{2,1,0:T(8,128)(2,1)S(1)}, bf16[1,128,2048]{2,1,0:T(8,128)(2,1)S(1)}, u32[]{:S(2)}, u32[]{:S(2)}) %collective-permute-start.19) | collective-permute-done | bytes 524320 | tf_op jit(solution)/shard_map/ppermute | solution.py:93
  227.6 6.5 copy.130
  234.3 21.0 %collective-permute-done.20 = bf16[2,128,2048]{2,1,0:T(8,128)(2,1)} collective-permute-done((bf16[2,128,2048]{2,1,0:T(8,128)(2,1)}, bf16[2,128,2048]{2,1,0:T(8,128)(2,1)}, u32[]{:S(2)}, u32[]{:S(2)}) %collective-permute-start.20) | collective-permute-done | bytes 1048608 | tf_op jit(solution)/shard_map/ppermute | solution.py:93
  263.3 6.1 fusion.62
  269.4 6.1 fusion.61
  275.5 11.0 %multiply_convert_fusion.7 = (bf16[1024,1024]{1,0:T(8,128)(2,1)}, bf16[1024,1024]{1,0:T(8,128)(2,1)}, bf16[1024,1024]{1,0:T(8,128)(2,1)}) fusion(f32[1024,1024]{1,0:T(8,128)} %fusion.61, f32[1024,1024]{1,0:T(8,128)} %fusion.62, bf16[1024,2048]{1,0:T(8,128)(2,1)S(1)} %bitcast.319, bf16[1024,2048]{1,0:T(8,128)(2,1)S(1)} %copy-done.47), kind=kOutput, calls=%fused_computation.15 | convolution fusion | flops 4311744512 | bytes 23068672 | tf_op jit(solution)/shard_map/dot_general | solution.py:23
  286.5 8.5 %fusion.63 = f32[1024,2048]{1,0:T(8,128)} fusion(bf16[1024,1024]{1,0:T(8,128)(2,1)} %get-tuple-element.28, bf16[1024,2048]{1,0:T(8,128)(2,1)S(1)} %copy-done.49), kind=kOutput, calls=%fused_computation.259 | convolution fusion | flops 4294967296 | bytes 14680064 | tf_op jit(solution)/shard_map/dot_general | solution.py:35
  294.9 6.9 %add_convert_fusion = bf16[1024,2048]{1,0:T(8,128)(2,1)S(1)} fusion(f32[1024,2048]{1,0:T(8,128)} %fusion.63, bf16[1024,1024]{1,0:T(8,128)(2,1)S(1)} %copy-done.58, bf16[1024,2048]{1,0:T(8,128)(2,1)S(1)} %copy-done.52), kind=kOutput, calls=%fused_computation.6 | convolution fusion | flops 4299161600 | bytes 18874368 | tf_op jit(solution)/shard_map/dot_general | solution.py:35
  315.5 18.0 %fusion.66 = f32[3072,1024]{1,0:T(8,128)} fusion(bf16[3072,2048]{1,0:T(8,128)(2,1)} %bitcast.304, bf16[1024,2048]{1,0:T(8,128)(2,1)S(1)} %copy-done.47), kind=kOutput, calls=%fused_computation.262 | convolution fusion | flops 12884901888 | bytes 29360128 | tf_op jit(solution)/shard_map/dot_general | solution.py:23
  337.9 9.6 %collective-permute-done.32 = bf16[1,128,2048]{2,1,0:T(8,128)(2,1)S(1)} collective-permute-done((bf16[1,128,2048]{2,1,0:T(8,128)(2,1)S(1)}, bf16[1,128,2048]{2,1,0:T(8,128)(2,1)S(1)}, u32[]{:S(2)}, u32[]{:S(2)}) %collective-permute-start.32) | collective-permute-done | bytes 524320 | tf_op jit(solution)/shard_map/ppermute | solution.py:93
  370.0 20.8 %shard_map.222 = (bf16[1024,256]{1,0:T(8,128)(2,1)}, bf16[1024,64]{1,0:T(8,128)(2,1)}, bf16[1024,64]{1,0:T(8,128)(2,1)}) custom-call(s32[8]{0:T(128)} %get-tuple-element.100.place_ref, s32[8]{0:T(128)} %bitcast.331, bf16[1024,256]{1,0:T(8,128)(2,1)} %maximum_multiply_fusion.q_ref, bf16[1024,64]{1,0:T(8,128)(2,1)} %pad_maximum_fusion.15.k_ref, ...), custom_call_target="tpu_custom_call" | custom-call | flops 2684354560 | bytes 4194304 | tf_op jit(solution)/shard_map/pallas_call | solution.py:318
  397.4 5.9 multiply_reduce_fusion
  424.9 12.9 %collective-permute-done.54 = bf16[128,2048]{1,0:T(8,128)(2,1)S(1)} collective-permute-done((bf16[128,2048]{1,0:T(8,128)(2,1)}, bf16[128,2048]{1,0:T(8,128)(2,1)S(1)}, u32[]{:S(2)}, u32[]{:S(2)}) %collective-permute-start.54) | collective-permute-done | bytes 524320 | tf_op jit(solution)/shard_map/ppermute | solution.py:124
  442.8 11.7 %collective-permute-done.55 = bf16[128,2048]{1,0:T(8,128)(2,1)S(1)} collective-permute-done((bf16[128,2048]{1,0:T(8,128)(2,1)S(1)}, bf16[128,2048]{1,0:T(8,128)(2,1)S(1)}, u32[]{:S(2)}, u32[]{:S(2)}) %collective-permute-start.55) | collective-permute-done | bytes 524320 | tf_op jit(solution)/shard_map/ppermute | solution.py:124
  462.9 13.7 %collective-permute-done.63 = f32[2,2048]{1,0:T(2,128)S(1)} collective-permute-done((f32[2,2048]{1,0:T(2,128)S(1)}, f32[2,2048]{1,0:T(2,128)S(1)}, u32[]{:S(2)}, u32[]{:S(2)}) %collective-permute-start.63) | collective-permute-done | bytes 16416 | tf_op jit(solution)/shard_map/ppermute | solution.py:164
  483.3 10.8 %collective-permute-done.44 = bf16[64,2048]{1,0:T(8,128)(2,1)S(1)} collective-permute-done((bf16[64,2048]{1,0:T(8,128)(2,1)S(1)}, bf16[64,2048]{1,0:T(8,128)(2,1)S(1)}, u32[]{:S(2)}, u32[]{:S(2)}) %collective-permute-start.44) | collective-permute-done | bytes 262176 | tf_op jit(solution)/shard_map/ppermute | solution.py:150
  494.3 8.3 %collective-permute-done.37 = bf16[96,2048]{1,0:T(8,128)(2,1)S(1)} collective-permute-done((bf16[96,2048]{1,0:T(8,128)(2,1)S(1)}, bf16[96,2048]{1,0:T(8,128)(2,1)S(1)}, u32[]{:S(2)}, u32[]{:S(2)}) %collective-permute-start.37) | collective-permute-done | bytes 393248 | tf_op jit(solution)/shard_map/ppermute | solution.py:150
  511.4 7.2 %collective-permute-done.57 = bf16[2,384,2048]{2,1,0:T(8,128)(2,1)S(1)} collective-permute-done((bf16[2,384,2048]{2,1,0:T(8,128)(2,1)S(1)}, bf16[2,384,2048]{2,1,0:T(8,128)(2,1)S(1)}, u32[]{:S(2)}, u32[]{:S(2)}) %collective-permute-start.57) | collective-permute-done | bytes 3145760 | tf_op jit(solution)/shard_map/ppermute | solution.py:93
  519.6 10.3 %collective-permute-done.34 = bf16[2,128,2048]{2,1,0:T(8,128)(2,1)S(1)} collective-permute-done((bf16[2,128,2048]{2,1,0:T(8,128)(2,1)S(1)}, bf16[2,128,2048]{2,1,0:T(8,128)(2,1)S(1)}, u32[]{:S(2)}, u32[]{:S(2)}) %collective-permute-start.34) | collective-permute-done | bytes 1048608 | tf_op jit(solution)/shard_map/ppermute | solution.py:93
  550.2 18.6 %fusion.68 = f32[3072,1024]{1,0:T(8,128)} fusion(bf16[3072,2048]{1,0:T(8,128)(2,1)} %bitcast.306, bf16[1024,2048]{1,0:T(8,128)(2,1)S(1)} %copy-done.50), kind=kOutput, calls=%fused_computation.264 | convolution fusion | flops 12884901888 | bytes 29360128 | tf_op jit(solution)/shard_map/dot_general | solution.py:23
  568.8 15.6 %fusion.67 = f32[3072,1024]{1,0:T(8,128)} fusion(bf16[3072,2048]{1,0:T(8,128)(2,1)S(1)} %bitcast.309, bf16[1024,2048]{1,0:T(8,128)(2,1)S(1)} %copy-done.53), kind=kOutput, calls=%fused_computation.263 | convolution fusion | flops 12884901888 | bytes 29360128 | tf_op jit(solution)/shard_map/dot_general | solution.py:23
  584.4 24.6 %fusion = f32[1024,2048]{1,0:T(8,128)} fusion(bf16[3072,2048]{1,0:T(8,128)(2,1)} %bitcast.307, f32[3072,1024]{1,0:T(8,128)} %fusion.66, f32[3072,1024]{1,0:T(8,128)} %fusion.68), kind=kOutput, calls=%fused_computation.9 | convolution fusion | flops 12903776256 | bytes 46137344 | tf_op jit(solution)/shard_map/dot_general | solution.py:29
  609.0 27.0 %fusion.2 = f32[1024,2048]{1,0:T(8,128)} fusion(bf16[3072,2048]{1,0:T(8,128)(2,1)} %bitcast.308, f32[3072,1024]{1,0:T(8,128)} %fusion.68, f32[3072,1024]{1,0:T(8,128)} %fusion.66, f32[3072,1024]{1,0:T(8,128)} %fusion.67), kind=kOutput, calls=%fused_computation.11 | convolution fusion | flops 12916359168 | bytes 58720256 | tf_op jit(solution)/shard_map/dot_general | solution.py:29
  636.0 24.6 %fusion.1 = f32[1024,2048]{1,0:T(8,128)} fusion(bf16[3072,2048]{1,0:T(8,128)(2,1)} %bitcast.305, f32[3072,1024]{1,0:T(8,128)} %fusion.67, f32[3072,1024]{1,0:T(8,128)} %fusion.68), kind=kOutput, calls=%fused_computation.10 | convolution fusion | flops 12903776256 | bytes 46137344 | tf_op jit(solution)/shard_map/dot_general | solution.py:29
  660.7 10.6 %convolution_add_fusion.1 = f32[1024,2048]{1,0:T(8,128)} fusion(f32[1024,2048]{1,0:T(8,128)} %fusion, bf16[1024,1024]{1,0:T(8,128)(2,1)S(1)} %copy-done.59, bf16[1024,2048]{1,0:T(8,128)(2,1)} %bitcast.323), kind=kOutput, calls=%fused_computation.20 | convolution fusion | flops 4297064448 | bytes 23068672 | tf_op jit(solution)/shard_map/dot_general | solution.py:29
  672.6 7.1 %convolution_add_fusion = f32[1024,2048]{1,0:T(8,128)} fusion(f32[1024,2048]{1,0:T(8,128)S(1)} %copy-done.54, bf16[1024,1024]{1,0:T(8,128)(2,1)S(1)} %copy-done.57, bf16[1024,2048]{1,0:T(8,128)(2,1)S(1)} %bitcast.320), kind=kOutput, calls=%fused_computation.19 | convolution fusion | flops 4297064448 | bytes 23068672 | tf_op jit(solution)/shard_map/dot_general | solution.py:29
  679.7 7.1 %convolution_add_fusion.2 = f32[1024,2048]{1,0:T(8,128)} fusion(f32[1024,2048]{1,0:T(8,128)S(1)} %bitcast.334, bf16[1024,1024]{1,0:T(8,128)(2,1)S(1)} %copy-done.55, bf16[1024,2048]{1,0:T(8,128)(2,1)S(1)} %bitcast.324), kind=kOutput, calls=%fused_computation.21 | convolution fusion | flops 4297064448 | bytes 23068672 | tf_op jit(solution)/shard_map/dot_general | solution.py:29
  (441 shorter events, 254.6 us)
Async XLA Ops:
  4.8 54.2 %collective-permute-start.12 = (bf16[64,2048]{1,0:T(8,128)(2,1)}, bf16[64,2048]{1,0:T(8,128)(2,1)S(1)}, u32[]{:S(2)}, u32[]{:S(2)}) collective-permute-start(bf16[64,2048]{1,0:T(8,128)(2,1)} %param.19), channel_id=1, source_target_pairs={{0,1},{1,2},{2,3},{3,0},{4,5},{5,6},{6,7},{7,4},{8,9},{9,10},{10,1... | collective-permute-start | bytes 786440 | tf_op jit(solution)/shard_map/ppermute | solution.py:124
  7.6 54.8 %collective-permute-start.9 = (bf16[96,2048]{1,0:T(8,128)(2,1)S(1)}, bf16[96,2048]{1,0:T(8,128)(2,1)}, u32[]{:S(2)}, u32[]{:S(2)}) collective-permute-start(bf16[96,2048]{1,0:T(8,128)(2,1)S(1)} %constant_dynamic-update-slice_fusion.7), channel_id=1, source_target_pairs={{0,1},{1,2},{2,3},{3,0},{4,5},{5,6},{6,7},{7,4},{8,9},{9,10},{10,1... | collective-permute-start | bytes 1179656 | tf_op jit(solution)/shard_map/ppermute | solution.py:124
  10.6 71.4 %collective-permute-start.26 = (bf16[1,128,2048]{2,1,0:T(8,128)(2,1)}, bf16[1,128,2048]{2,1,0:T(8,128)(2,1)S(1)}, u32[]{:S(2)}, u32[]{:S(2)}) collective-permute-start(bf16[1,128,2048]{2,1,0:T(8,128)(2,1)} %param.25), channel_id=1, source_target_pairs={{0,8},{4,20},{8,0},{12,28},{16,24},{20,4},{24,16},{28,12},{1,9},{5... | collective-permute-start | bytes 1572872 | tf_op jit(solution)/shard_map/ppermute | solution.py:93
  12.1 68.8 %collective-permute-start = (bf16[1,128,2048]{2,1,0:T(8,128)(2,1)}, bf16[1,128,2048]{2,1,0:T(8,128)(2,1)S(1)}, u32[]{:S(2)}, u32[]{:S(2)}) collective-permute-start(bf16[1,128,2048]{2,1,0:T(8,128)(2,1)} %param.14), channel_id=1, source_target_pairs={{0,8},{4,20},{8,0},{12,28},{16,24},{20,4},{24,16},{28,12},{1,9},{5... | collective-permute-start | bytes 1572872 | tf_op jit(solution)/shard_map/ppermute | solution.py:93
  30.3 28.2 %collective-permute-start.8 = (bf16[2,2048]{1,0:T(2,128)(2,1)S(1)}, bf16[2,2048]{1,0:T(2,128)(2,1)S(1)}, u32[]{:S(2)}, u32[]{:S(2)}) collective-permute-start(bf16[2,2048]{1,0:T(2,128)(2,1)S(1)} %add.375), channel_id=1, source_target_pairs={{0,16},{4,20},{8,24},{12,28},{16,0},{20,4},{24,8},{28,12},{1,17},{... | collective-permute-start | bytes 24584 | tf_op jit(solution)/shard_map/ppermute | solution.py:164
  58.6 25.1 %collective-permute-start.46 = (bf16[128,2048]{1,0:T(8,128)(2,1)S(1)}, bf16[128,2048]{1,0:T(8,128)(2,1)S(1)}, u32[]{:S(2)}, u32[]{:S(2)}) collective-permute-start(bf16[128,2048]{1,0:T(8,128)(2,1)S(1)} %bitcast.270), channel_id=1, source_target_pairs={{0,1},{1,2},{2,3},{3,0},{4,5},{5,6},{6,7},{7,4},{8,9},{9,10},{10,1... | collective-permute-start | bytes 1572872 | tf_op jit(solution)/shard_map/ppermute | solution.py:124
  62.4 31.5 %collective-permute-start.10 = (bf16[96,2048]{1,0:T(8,128)(2,1)}, bf16[96,2048]{1,0:T(8,128)(2,1)S(1)}, u32[]{:S(2)}, u32[]{:S(2)}) collective-permute-start(bf16[96,2048]{1,0:T(8,128)(2,1)} %collective-permute-done.9), channel_id=1, source_target_pairs={{0,1},{1,2},{2,3},{3,0},{4,5},{5,6},{6,7},{7,4},{8,9},{9,10},{10,1... | collective-permute-start | bytes 1179656 | tf_op jit(solution)/shard_map/ppermute | solution.py:124
  82.0 50.5 %collective-permute-start.2 = (bf16[2,128,2048]{2,1,0:T(8,128)(2,1)}, bf16[2,128,2048]{2,1,0:T(8,128)(2,1)S(1)}, u32[]{:S(2)}, u32[]{:S(2)}) collective-permute-start(bf16[2,128,2048]{2,1,0:T(8,128)(2,1)} %get-tuple-element.65), channel_id=1, source_target_pairs={{0,4},{4,0},{8,12},{12,8},{16,20},{20,16},{24,28},{28,24},{1,5},{5... | collective-permute-start | bytes 3145736 | tf_op jit(solution)/shard_map/ppermute | solution.py:93
  82.0 34.6 %collective-permute-start.1 = (bf16[2,128,2048]{2,1,0:T(8,128)(2,1)}, bf16[2,128,2048]{2,1,0:T(8,128)(2,1)S(1)}, u32[]{:S(2)}, u32[]{:S(2)}) collective-permute-start(bf16[2,128,2048]{2,1,0:T(8,128)(2,1)} %get-tuple-element.65), channel_id=1, source_target_pairs={{0,16},{4,12},{8,24},{12,4},{16,0},{20,28},{24,8},{28,20},{1,17},{... | collective-permute-start | bytes 3145736 | tf_op jit(solution)/shard_map/ppermute | solution.py:93
  83.7 45.0 %collective-permute-start.27 = (bf16[2,128,2048]{2,1,0:T(8,128)(2,1)}, bf16[2,128,2048]{2,1,0:T(8,128)(2,1)}, u32[]{:S(2)}, u32[]{:S(2)}) collective-permute-start(bf16[2,128,2048]{2,1,0:T(8,128)(2,1)} %get-tuple-element.61), channel_id=1, source_target_pairs={{0,16},{4,12},{8,24},{12,4},{16,0},{20,28},{24,8},{28,20},{1,17},{... | collective-permute-start | bytes 3145736 | tf_op jit(solution)/shard_map/ppermute | solution.py:93
  109.2 23.4 %collective-permute-start.15 = (bf16[1,256,2048]{2,1,0:T(8,128)(2,1)S(1)}, bf16[1,256,2048]{2,1,0:T(8,128)(2,1)S(1)}, u32[]{:S(2)}, u32[]{:S(2)}) collective-permute-start(bf16[1,256,2048]{2,1,0:T(8,128)(2,1)S(1)} %bitcast.261), channel_id=1, source_target_pairs={{0,8},{4,20},{8,0},{12,28},{16,24},{20,4},{24,16},{28,12},{1,9},{5... | collective-permute-start | bytes 3145736 | tf_op jit(solution)/shard_map/ppermute | solution.py:93
  127.4 43.5 %collective-permute-start.28 = (bf16[2,128,2048]{2,1,0:T(8,128)(2,1)}, bf16[2,128,2048]{2,1,0:T(8,128)(2,1)}, u32[]{:S(2)}, u32[]{:S(2)}) collective-permute-start(bf16[2,128,2048]{2,1,0:T(8,128)(2,1)} %get-tuple-element.61), channel_id=1, source_target_pairs={{0,4},{4,0},{8,12},{12,8},{16,20},{20,16},{24,28},{28,24},{1,5},{5... | collective-permute-start | bytes 3145736 | tf_op jit(solution)/shard_map/ppermute | solution.py:93
  128.7 61.7 %collective-permute-start.49 = (bf16[1,384,2048]{2,1,0:T(8,128)(2,1)}, bf16[1,384,2048]{2,1,0:T(8,128)(2,1)}, u32[]{:S(2)}, u32[]{:S(2)}) collective-permute-start(bf16[1,384,2048]{2,1,0:T(8,128)(2,1)} %maximum_bitcast_fusion), channel_id=1, source_target_pairs={{0,8},{4,20},{8,0},{12,28},{16,24},{20,4},{24,16},{28,12},{1,9},{5... | collective-permute-start | bytes 4718600 | tf_op jit(solution)/shard_map/ppermute | solution.py:93
  132.5 49.6 %collective-permute-start.29 = (bf16[2,128,2048]{2,1,0:T(8,128)(2,1)}, bf16[2,128,2048]{2,1,0:T(8,128)(2,1)}, u32[]{:S(2)}, u32[]{:S(2)}) collective-permute-start(bf16[2,128,2048]{2,1,0:T(8,128)(2,1)} %collective-permute-done.27), channel_id=1, source_target_pairs={{0,4},{4,0},{8,12},{12,8},{16,20},{20,16},{24,28},{28,24},{1,5},{5... | collective-permute-start | bytes 3145736 | tf_op jit(solution)/shard_map/ppermute | solution.py:93
  134.2 46.9 %collective-permute-start.16 = (bf16[2,256,2048]{2,1,0:T(8,128)(2,1)}, bf16[2,256,2048]{2,1,0:T(8,128)(2,1)}, u32[]{:S(2)}, u32[]{:S(2)}) collective-permute-start(bf16[2,256,2048]{2,1,0:T(8,128)(2,1)} %pad_maximum_fusion.3), channel_id=1, source_target_pairs={{0,16},{4,12},{8,24},{12,4},{16,0},{20,28},{24,8},{28,20},{1,17},{... | collective-permute-start | bytes 6291464 | tf_op jit(solution)/shard_map/ppermute | solution.py:93
  173.2 27.8 %collective-permute-start.17 = (bf16[2,256,2048]{2,1,0:T(8,128)(2,1)}, bf16[2,256,2048]{2,1,0:T(8,128)(2,1)}, u32[]{:S(2)}, u32[]{:S(2)}) collective-permute-start(bf16[2,256,2048]{2,1,0:T(8,128)(2,1)} %pad_maximum_fusion.3), channel_id=1, source_target_pairs={{0,4},{4,0},{8,12},{12,8},{16,20},{20,16},{24,28},{28,24},{1,5},{5... | collective-permute-start | bytes 6291464 | tf_op jit(solution)/shard_map/ppermute | solution.py:93
  181.1 23.6 %collective-permute-start.18 = (bf16[2,256,2048]{2,1,0:T(8,128)(2,1)}, bf16[2,256,2048]{2,1,0:T(8,128)(2,1)S(1)}, u32[]{:S(2)}, u32[]{:S(2)}) collective-permute-start(bf16[2,256,2048]{2,1,0:T(8,128)(2,1)} %collective-permute-done.16), channel_id=1, source_target_pairs={{0,4},{4,0},{8,12},{12,8},{16,20},{20,16},{24,28},{28,24},{1,5},{5... | collective-permute-start | bytes 6291464 | tf_op jit(solution)/shard_map/ppermute | solution.py:93
  194.5 107.8 %collective-permute-start.51 = (bf16[2,384,2048]{2,1,0:T(8,128)(2,1)}, bf16[2,384,2048]{2,1,0:T(8,128)(2,1)}, u32[]{:S(2)}, u32[]{:S(2)}) collective-permute-start(bf16[2,384,2048]{2,1,0:T(8,128)(2,1)} %pad_maximum_fusion.1), channel_id=1, source_target_pairs={{0,4},{4,0},{8,12},{12,8},{16,20},{20,16},{24,28},{28,24},{1,5},{5... | collective-permute-start | bytes 9437192 | tf_op jit(solution)/shard_map/ppermute | solution.py:93
  194.5 61.8 %collective-permute-start.50 = (bf16[2,384,2048]{2,1,0:T(8,128)(2,1)}, bf16[2,384,2048]{2,1,0:T(8,128)(2,1)}, u32[]{:S(2)}, u32[]{:S(2)}) collective-permute-start(bf16[2,384,2048]{2,1,0:T(8,128)(2,1)} %pad_maximum_fusion.1), channel_id=1, source_target_pairs={{0,16},{4,12},{8,24},{12,4},{16,0},{20,28},{24,8},{28,20},{1,17},{... | collective-permute-start | bytes 9437192 | tf_op jit(solution)/shard_map/ppermute | solution.py:93
  226.0 29.3 %collective-permute-start.20 = (bf16[2,128,2048]{2,1,0:T(8,128)(2,1)}, bf16[2,128,2048]{2,1,0:T(8,128)(2,1)}, u32[]{:S(2)}, u32[]{:S(2)}) collective-permute-start(bf16[2,128,2048]{2,1,0:T(8,128)(2,1)} %pad_maximum_fusion.9), channel_id=1, source_target_pairs={{0,16},{4,12},{8,24},{12,4},{16,0},{20,28},{24,8},{28,20},{1,17},{... | collective-permute-start | bytes 3145736 | tf_op jit(solution)/shard_map/ppermute | solution.py:93
  234.2 28.1 %collective-permute-start.21 = (bf16[2,128,2048]{2,1,0:T(8,128)(2,1)}, bf16[2,128,2048]{2,1,0:T(8,128)(2,1)S(1)}, u32[]{:S(2)}, u32[]{:S(2)}) collective-permute-start(bf16[2,128,2048]{2,1,0:T(8,128)(2,1)} %pad_maximum_fusion.9), channel_id=1, source_target_pairs={{0,4},{4,0},{8,12},{12,8},{16,20},{20,16},{24,28},{28,24},{1,5},{5... | collective-permute-start | bytes 3145736 | tf_op jit(solution)/shard_map/ppermute | solution.py:93
  256.4 55.6 %collective-permute-start.52 = (bf16[2,384,2048]{2,1,0:T(8,128)(2,1)}, bf16[2,384,2048]{2,1,0:T(8,128)(2,1)S(1)}, u32[]{:S(2)}, u32[]{:S(2)}) collective-permute-start(bf16[2,384,2048]{2,1,0:T(8,128)(2,1)} %collective-permute-done.50), channel_id=1, source_target_pairs={{0,4},{4,0},{8,12},{12,8},{16,20},{20,16},{24,28},{28,24},{1,5},{5... | collective-permute-start | bytes 9437192 | tf_op jit(solution)/shard_map/ppermute | solution.py:93
  360.4 179.5 %collective-permute-start.25 = (bf16[1,128,2048]{2,1,0:T(8,128)(2,1)}, bf16[1,128,2048]{2,1,0:T(8,128)(2,1)}, u32[]{:S(2)}, u32[]{:S(2)}) collective-permute-start(bf16[1,128,2048]{2,1,0:T(8,128)(2,1)} %slice.356), channel_id=1, source_target_pairs={{0,8},{4,20},{8,0},{12,28},{16,24},{20,4},{24,16},{28,12},{1,9},{5... | collective-permute-start | bytes 1572872 | tf_op jit(solution)/shard_map/ppermute | solution.py:93
  362.3 59.2 %collective-permute-start.53 = (bf16[128,2048]{1,0:T(8,128)(2,1)}, bf16[128,2048]{1,0:T(8,128)(2,1)}, u32[]{:S(2)}, u32[]{:S(2)}) collective-permute-start(bf16[128,2048]{1,0:T(8,128)(2,1)} %get-tuple-element.42), channel_id=1, source_target_pairs={{0,1},{1,2},{2,3},{3,0},{4,5},{5,6},{6,7},{7,4},{8,9},{9,10},{10,1... | collective-permute-start | bytes 1572872 | tf_op jit(solution)/shard_map/ppermute | solution.py:124
  365.6 37.8 %all-to-all-start.2 = ((bf16[8,128,256]{2,1,0:T(8,128)(2,1)}), bf16[8,128,256]{2,1,0:T(8,128)(2,1)}, u32[]{:S(2)}, u32[]{:S(2)}) async-start(bf16[8,128,256]{2,1,0:T(8,128)(2,1)} %fusion.39), calls=%async_computation.2 | async-start | bytes 1048576 | tf_op jit(solution)/shard_map/all_to_all | solution.py:545
  403.4 36.7 %collective-permute-start.60 = (f32[2,2048]{1,0:T(2,128)S(1)}, f32[2,2048]{1,0:T(2,128)S(1)}, u32[]{:S(2)}, u32[]{:S(2)}) collective-permute-start(f32[2,2048]{1,0:T(2,128)S(1)} %pad_maximum_fusion.16), channel_id=1, source_target_pairs={{0,1},{1,0},{2,3},{3,2},{4,5},{5,4},{6,7},{7,6},{8,9},{9,8},{10,11... | collective-permute-start | bytes 49160 | tf_op jit(solution)/shard_map/ppermute | solution.py:160
  438.1 44.9 %collective-permute-start.43 = (bf16[64,2048]{1,0:T(8,128)(2,1)S(1)}, bf16[64,2048]{1,0:T(8,128)(2,1)S(1)}, u32[]{:S(2)}, u32[]{:S(2)}) collective-permute-start(bf16[64,2048]{1,0:T(8,128)(2,1)S(1)} %fusion.41), channel_id=1, source_target_pairs={{0,1},{1,2},{2,3},{3,0},{4,5},{5,6},{6,7},{7,4},{8,9},{9,10},{10,1... | collective-permute-start | bytes 786440 | tf_op jit(solution)/shard_map/ppermute | solution.py:150
  455.8 25.3 %collective-permute-start.56 = (bf16[1,384,2048]{2,1,0:T(8,128)(2,1)S(1)}, bf16[1,384,2048]{2,1,0:T(8,128)(2,1)S(1)}, u32[]{:S(2)}, u32[]{:S(2)}) collective-permute-start(bf16[1,384,2048]{2,1,0:T(8,128)(2,1)S(1)} %maximum_bitcast_fusion.1), channel_id=1, source_target_pairs={{0,8},{4,20},{8,0},{12,28},{16,24},{20,4},{24,16},{28,12},{1,9},{5... | collective-permute-start | bytes 4718600 | tf_op jit(solution)/shard_map/ppermute | solution.py:93
  481.3 37.3 %collective-permute-start.57 = (bf16[2,384,2048]{2,1,0:T(8,128)(2,1)S(1)}, bf16[2,384,2048]{2,1,0:T(8,128)(2,1)S(1)}, u32[]{:S(2)}, u32[]{:S(2)}) collective-permute-start(bf16[2,384,2048]{2,1,0:T(8,128)(2,1)S(1)} %pad_maximum_fusion.2), channel_id=1, source_target_pairs={{0,16},{4,12},{8,24},{12,4},{16,0},{20,28},{24,8},{28,20},{1,17},{... | collective-permute-start | bytes 9437192 | tf_op jit(solution)/shard_map/ppermute | solution.py:93
  503.7 26.2 %collective-permute-start.34 = (bf16[2,128,2048]{2,1,0:T(8,128)(2,1)S(1)}, bf16[2,128,2048]{2,1,0:T(8,128)(2,1)S(1)}, u32[]{:S(2)}, u32[]{:S(2)}) collective-permute-start(bf16[2,128,2048]{2,1,0:T(8,128)(2,1)S(1)} %slice.351), channel_id=1, source_target_pairs={{0,16},{4,12},{8,24},{12,4},{16,0},{20,28},{24,8},{28,20},{1,17},{... | collective-permute-start | bytes 3145736 | tf_op jit(solution)/shard_map/ppermute | solution.py:93
  511.4 33.5 %collective-permute-start.58 = (bf16[2,384,2048]{2,1,0:T(8,128)(2,1)S(1)}, bf16[2,384,2048]{2,1,0:T(8,128)(2,1)S(1)}, u32[]{:S(2)}, u32[]{:S(2)}) collective-permute-start(bf16[2,384,2048]{2,1,0:T(8,128)(2,1)S(1)} %pad_maximum_fusion.2), channel_id=1, source_target_pairs={{0,4},{4,0},{8,12},{12,8},{16,20},{20,16},{24,28},{28,24},{1,5},{5... | collective-permute-start | bytes 9437192 | tf_op jit(solution)/shard_map/ppermute | solution.py:93
  518.6 28.2 %collective-permute-start.59 = (bf16[2,384,2048]{2,1,0:T(8,128)(2,1)S(1)}, bf16[2,384,2048]{2,1,0:T(8,128)(2,1)S(1)}, u32[]{:S(2)}, u32[]{:S(2)}) collective-permute-start(bf16[2,384,2048]{2,1,0:T(8,128)(2,1)S(1)} %collective-permute-done.57), channel_id=1, source_target_pairs={{0,4},{4,0},{8,12},{12,8},{16,20},{20,16},{24,28},{28,24},{1,5},{5... | collective-permute-start | bytes 9437192 | tf_op jit(solution)/shard_map/ppermute | solution.py:93
  (100 other events, 1463.3 us)
